TPU v7x, 256 devices: a whole 4x4x8 slice. The times are simulated.
256 devices in a mesh: tm: 16 (over y_hi, z), batch: 8 (over x, core), width: 2 (over y_lo).
Axes of the slice: x: 4, y: 4 (y_hi: 2, y_lo: 2; y = y_hi * 2 + y_lo), z: 8, core: 2. Of those that a mesh axis runs over, the one named last changes fastest.
Arguments:
- moves: int32 [16, 4096], P('batch', 'tm'), may hold values from 0 to 361
- lengths: int32 [16], P('batch'), may hold values from 1 to 4096
- outcomes: int32 [16], P('batch'), may hold values from -1 to 1
- embedded: bfloat16 [16, 4096, 2048], P('batch', 'tm', 'width'), may hold values from -6 to 6
- w_branches: bfloat16 [4, 2048, 2048], P(None, ('tm', 'batch'), 'width'), may hold values from -0.125 to 0.125
- conv_w: float32 [4, 2048], P(None, 'width'), may hold values from -3 to 3
- gate_bias: float32 [2, 2048], P(None, 'width'), may hold values from -4 to 4
- rates: float32 [2048], P('width'), may hold values from 0.001 to 0.105
- w_down: bfloat16 [2048, 2048], P(('tm', 'batch'), 'width'), may hold values from -0.125 to 0.125
- w_policy: bfloat16 [2048, 362], P('width'), may hold values from -12 to 12
- w_value: bfloat16 [2048], P('width'), may hold values from -0.125 to 0.125
Outputs:
- position_loss: float32 [16, 4096], P('batch', 'tm')
- value: float32 [16, 4096], P('batch', 'tm')
All inputs are finite; a program needn't handle non-finite values.
Results may differ from a plain program's by a relative error of at most 0.0033.
Values may be sent and summed in bfloat16 or wider, within the bound.
No kernel may reach another device: no remote copies, remote signals or barrier semaphores. Data moves between devices by JAX's collectives and lax.ppermute only.
A program may use at most 128 MiB of HBM per device.

v0:
```python
import jax
import jax.numpy as jnp
from jax import lax
from jax.sharding import PartitionSpec as P

D = 2048
KERNEL = 4


def from_behind(value, axis, steps):
    count = lax.axis_size(axis)
    initial, last = (max(0, -steps), min(count, count - steps))
    return lax.ppermute(value, axis, [(source, source + steps) for source in range(initial, last)])


def collected_together(x, axis):
    leaves = jax.tree.leaves(x)
    turns = sorted(range(len(leaves)), key=lambda k: -leaves[k].size)
    width = (1, *leaves[turns[0]].shape)[-1]
    lines = [
        jnp.pad(leaves[k].reshape(-1), (0, -leaves[k].size % width)).reshape(-1, width)
        for k in turns
    ]
    both, at, found = (lax.all_gather(jnp.concatenate(lines), axis), 0, {})
    for k, line in zip(turns, lines):
        share = both[:, at : at + len(line)].reshape(len(both), -1)
        found[k] = share[:, : leaves[k].size].reshape(-1, *leaves[k].shape)
        at += len(line)
    numbers = iter(range(len(leaves)))
    return jax.tree.map(lambda _: found[next(numbers)], x)


def prefix(x, axis, combine, identity):
    length, here = (lax.axis_size(axis), lax.axis_index(axis))
    everything = collected_together(x, axis)
    start = jax.tree.map(
        lambda part, zero: jnp.broadcast_to(jnp.asarray(zero, part.dtype), part.shape), x, identity
    )

    def turn(k, before):
        reached = k < here
        new = combine(before, jax.tree.map(lambda part: part[k], everything))
        return jax.tree.map(lambda a, b: jnp.where(reached, a, b), new, before)

    return lax.fori_loop(0, length, turn, start)


def in_blocks(x, dim, length):
    lengths = x.shape
    pieces = x.reshape(*lengths[:dim], length, lengths[dim] // length, *lengths[dim + 1 :])
    return jnp.moveaxis(pieces, dim, 0)


def sum_at_owner(x, axis, dim):
    length = lax.axis_size(axis)
    pieces = lax.all_to_all(in_blocks(x, dim, length), axis, 0, 0, tiled=True)
    return jnp.sum(pieces, axis=0)


def sent_to_all(x, axis):
    length = lax.axis_size(axis)
    return lax.all_to_all(jnp.broadcast_to(x[None], (length, *x.shape)), axis, 0, 0, tiled=True)


def over_copies(x, axis):
    return sent_to_all(x, axis).sum(axis=0)


def packed_total(arrays, axis):
    ends = [0]
    for a in arrays:
        ends.append(ends[-1] + a.size)
    total = over_copies(jnp.concatenate([a.ravel() for a in arrays]), axis)
    return tuple((total[b:e].reshape(a.shape) for a, b, e in zip(arrays, ends, ends[1:])))


def link(early, late):
    return (early[0] + late[0], jnp.exp(late[0]) * early[1] + late[1])


def compose(early, late):
    return (early[0] * late[0], late[0] * early[1] + late[1])


def shards(
    moves,
    lengths,
    outcomes,
    embedded,
    w_branches,
    conv_w,
    gate_bias,
    rates,
    w_down,
    w_policy,
    w_value,
):
    games, block_len, half = embedded.shape
    count = games * block_len
    chans = w_branches.shape[2]
    features = lax.all_gather(embedded, "width", axis=2, tiled=True).reshape(count, -1)
    proj = jnp.einsum(
        "td,kdn->ktn",
        features,
        lax.all_gather(w_branches, ("tm", "batch"), axis=1, tiled=True),
        preferred_element_type=jnp.float32,
    )
    proj = proj.reshape(4, games, block_len, chans)
    gated = jax.nn.gelu(proj[0])
    source = proj[1]
    prior = from_behind(source[:, block_len - (KERNEL - 1) :, :], "tm", 1)
    extended = jnp.concatenate([prior, source], 1)
    conv = jnp.zeros((games, block_len, chans), jnp.float32)
    for k in range(KERNEL):
        conv = conv + conv_w[k] * extended[:, KERNEL - 1 - k : KERNEL - 1 - k + block_len]
    recur = jax.nn.sigmoid(proj[2] + gate_bias[0])
    inflow = jax.nn.sigmoid(proj[3] + gate_bias[1])
    log_a = -8.0 * recur * rates
    decay = jnp.exp(log_a)
    drive = jnp.sqrt(1.0 - decay * decay) * inflow * conv
    summed, local = lax.associative_scan(link, (log_a, drive), axis=1)
    block_decay = jnp.exp(summed[:, -1])
    block_end = local[:, -1]
    identity = (jnp.ones_like(block_decay), jnp.zeros_like(block_end))
    _, incoming = prefix((block_decay, block_end), "tm", compose, identity)
    hidden = local + jnp.exp(summed) * incoming[:, None, :]
    mixed = (hidden * gated).astype(jnp.bfloat16).reshape(count, chans)
    partial_down = lax.dot_general(
        mixed,
        lax.all_gather(w_down, ("tm", "batch"), axis=0, tiled=True),
        (((1,), (1,)), ((), ())),
        preferred_element_type=jnp.float32,
    )
    down = sum_at_owner(partial_down, "width", 1)
    resid = (embedded.reshape(count, half).astype(jnp.float32) + down).astype(jnp.bfloat16)
    wide = resid.astype(jnp.float32)
    local_sq = jnp.sum(wide * wide, -1)
    local_logits = jnp.dot(resid, w_policy, preferred_element_type=jnp.float32)
    local_value = jnp.dot(resid, w_value, preferred_element_type=jnp.float32)
    raw_logits, raw_value, sumsq = packed_total((local_logits, local_value, local_sq), "width")
    norm = lax.rsqrt(sumsq / D + 1e-06)
    logits = raw_logits * norm[:, None]
    value = jnp.tanh(raw_value * norm)
    top = jnp.max(logits, -1, keepdims=True)
    lse = top[:, 0] + jnp.log(jnp.sum(jnp.exp(logits - top), -1))
    column = lax.broadcasted_iota(jnp.int32, logits.shape, 1)
    picked = jnp.sum(jnp.where(column == moves.reshape(count, 1), logits, 0.0), -1)
    target = jnp.broadcast_to(outcomes.astype(jnp.float32)[:, None], (games, block_len)).reshape(
        count
    )
    position = lax.axis_index("tm") * block_len + lax.broadcasted_iota(
        jnp.int32, (games, block_len), 1
    )
    where_live = (position < lengths[:, None]).reshape(count)
    loss = jnp.where(where_live, lse - picked + (value - target) ** 2, 0.0)
    return (loss.reshape(games, block_len), value.reshape(games, block_len))


def solution(mesh):
    in_specs = (
        P("batch", "tm"),
        P("batch"),
        P("batch"),
        P("batch", "tm", "width"),
        P(None, ("tm", "batch"), "width"),
        P(None, "width"),
        P(None, "width"),
        P("width"),
        P(("tm", "batch"), "width"),
        P("width", None),
        P("width"),
    )
    out_specs = (P("batch", "tm"), P("batch", "tm"))
    return jax.shard_map(shards, mesh=mesh, in_specs=in_specs, out_specs=out_specs, check_vma=False)
```

profile of v0, /device:TPU:16, one launch (start us, length us, event | category | flops | bytes accessed | tf_op | source)
XLA Modules:
  0.0 543.8 jit_solution(808997594253362417)
XLA Ops:
  11.1 39.5 %all-gather.8.cloned.1.call-done = bf16[2,256,2048]{2,1,0:T(8,128)(2,1)} async-done(((bf16[2,256,1024]{2,1,0:T(8,128)(2,1)}), bf16[2,256,2048]{2,1,0:T(8,128)(2,1)}) %all-gather.8.cloned.1.call-update) | async-done | bytes 2097168 | tf_op jit(solution)/shard_map/all_gather | solution.py:101
  50.5 150.2 %all-gather.6.cloned.1.call-done = bf16[4,2048,1024]{2,1,0:T(8,128)(2,1)} async-done(((bf16[4,16,1024]{2,1,0:T(8,128)(2,1)}), bf16[4,2048,1024]{2,1,0:T(8,128)(2,1)}) %all-gather.6.cloned.1.call-update) | async-done | bytes 16777232 | tf_op jit(solution)/shard_map/all_gather | solution.py:105
  200.7 12.5 %convolution_bitcast_fusion = f32[4,512,1024]{2,1,0:T(8,128)S(1)} fusion(bf16[512,2048,1]{1,0,2:T(8,128)(2,1)} %bitcast.96, bf16[4,2048,1024]{2,1,0:T(8,128)(2,1)} %all-gather.6.cloned.1.call-done), kind=kOutput, calls=%fused_computation.3 | convolution fusion | flops 8589934592 | bytes 27262976 | tf_op jit(solution)/shard_map/td,kdn->ktn/dot_general | solution.py:102
  213.2 2.9 fusion.33
  217.5 3.5 collective-permute-start
  221.0 5.9 %collective-permute-done = f32[2,3,1024]{2,1,0:T(4,128)S(1)} collective-permute-done((f32[2,3,1024]{2,1,0:T(4,128)S(1)}, f32[2,3,1024]{2,1,0:T(4,128)S(1)}, u32[]{:S(2)}, u32[]{:S(2)}) %collective-permute-start) | collective-permute-done | bytes 24608 | tf_op jit(solution)/shard_map/ppermute | solution.py:13
  226.9 7.6 %fusion.5 = (f32[2,256,1024]{2,1,0:T(8,128)S(1)}, f32[2,256,1024]{2,1,0:T(8,128)}) fusion(f32[2,3,1024]{2,1,0:T(4,128)S(1)} %collective-permute-done, f32[2,256,1024]{2,1,0:T(8,128)} %bitcast.67, f32[2,256,1024]{2,1,0:T(8,128)} %bitcast.70, f32[1024]{0:T(1024)S(1)} %bitcast.88, f32[1024]{0:T(1024)S(1)} %bitcast.89, f32[1024]{0:T(1024)S(1)} %bitcast.87, ...), kind=kLoop, calls=%fused_computation.12 | loop fusion | flops 12058624 | bytes 10539008 | tf_op jit(solution)/shard_map/mul | solution.py:120
  234.5 2.9 slice.333
  237.4 2.9 slice.334
  240.3 5.4 slice.332
  245.7 5.4 slice.336
  251.1 4.1 multiply_add_fusion
  255.2 3.3 slice.339
  258.5 3.2 slice.340
  261.7 3.3 slice.338
  265.0 3.3 slice.342
  268.3 2.5 multiply_add_fusion.1
  272.3 1.7 slice.344
  274.0 1.7 slice.348
  275.7 2.0 multiply_add_fusion.2
  277.7 1.6 slice.351
  279.4 1.6 slice.352
  281.0 1.6 slice.350
  282.6 1.6 slice.354
  284.2 1.8 multiply_add_fusion.3
  287.3 1.5 slice.356
  288.9 1.5 slice.360
  290.4 1.6 multiply_add_fusion.4
  304.7 1.5 fusion.35
  307.1 1.5 slice.378
  311.4 1.5 slice.355
  316.6 1.6 slice.382
  321.2 1.7 slice.343
  325.7 3.3 slice.337
  329.0 3.3 slice.386
  335.2 5.6 %slice.331 = f32[2,127,1024]{2,1,0:T(8,128)} slice(f32[2,256,1024]{2,1,0:T(8,128)} %get-tuple-element.128), slice={[0:2:1], [2:256:2], [0:1024:1]} | slice | bytes 2080768 | tf_op jit(solution)/shard_map/slice | solution.py:121
  340.8 2.9 slice.388
  343.8 1.5 slice.446
  356.1 5.4 pad.129
  361.4 2.0 pad_maximum_fusion.4
  363.4 3.0 pad.110
  366.4 2.0 pad.111
  368.4 2.9 add.346
  371.3 2.9 fusion.20
  375.3 5.4 pad.128
  381.6 5.4 pad.113
  386.9 2.3 pad_maximum_fusion.1
  389.3 5.5 %pad.112 = f32[2,256,1024]{2,1,0:T(8,128)} pad(f32[2,128,1024]{2,1,0:T(8,128)} %pad_maximum_fusion.1, f32[]{:T(128)} %constant.43.clone.1), padding=0_0_0x0_1_1x0_0_0 | pad | bytes 3145732 | tf_op jit(solution)/shard_map/pad | solution.py:121
  395.6 37.9 %all-gather.1 = f32[16,4,1024]{2,1,0:T(4,128)S(1)} all-gather(f32[1,4,1024]{2,1,0:T(4,128)S(1)} %maximum_bitcast_fusion), channel_id=2, replica_groups=mesh['tm'=16,'batch'=8,'width'=2] {'tm'}, dimensions={0}, use_global_device_ids=true | all-gather | bytes 278528 | tf_op jit(solution)/shard_map/all_gather | solution.py:24
  434.4 5.8 %fusion.17 = bf16[2,256,1024]{2,1,0:T(8,128)(2,1)} fusion(f32[2,256,1024]{2,1,0:T(8,128)} %bitcast.68, f32[2,256,1024]{2,1,0:T(8,128)} %pad.128, f32[2,256,1024]{2,1,0:T(8,128)S(1)} %copy-done.4, f32[2,256,1024]{2,1,0:T(8,128)} %pad.112, f32[2,256,1024]{2,1,0:T(8,128)} %pad.113, f32[2,1024]{1,0:T(2,128)S(1)} %get-tuple-element.96), kind=kLoop, calls=%fused_computation.24 | loop fusion | flops 7340032 | bytes 11542528 | tf_op jit(solution)/shard_map/convert_element_type | solution.py:127
  440.1 6.9 %convolution_bitcast_fusion.1 = f32[2,512,1024]{2,1,0:T(8,128)} fusion(bf16[512,1024,1]{1,0,2:T(8,128)(2,1)} %bitcast.71, bf16[2,1024,1024]{2,1,0:T(8,128)(2,1)} %bitcast.95), kind=kOutput, calls=%fused_computation.7 | convolution fusion | flops 2147483648 | bytes 9437184 | tf_op jit(solution)/shard_map/dot_general | solution.py:128
  447.0 5.8 %all-to-all-start = ((f32[2,512,1024]{2,1,0:T(8,128)}), f32[2,512,1024]{2,1,0:T(8,128)}, u32[]{:S(2)}, u32[]{:S(2)}) async-start(f32[2,512,1024]{2,1,0:T(8,128)} %convolution_bitcast_fusion.1), calls=%async_computation | async-start | bytes 8388608 | tf_op jit(solution)/shard_map/all_to_all | solution.py:56
  452.8 40.3 %all-to-all-done = f32[2,512,1024]{2,1,0:T(8,128)} async-done(((f32[2,512,1024]{2,1,0:T(8,128)}), f32[2,512,1024]{2,1,0:T(8,128)}, u32[]{:S(2)}, u32[]{:S(2)}) %all-to-all-start) | async-done | bytes 4194336 | tf_op jit(solution)/shard_map/all_to_all | solution.py:56
  493.1 2.8 reduce_sum.49
  495.9 1.6 fusion.19
  498.5 1.6 fusion.39
  500.1 2.8 reshape.100
  502.9 1.7 fusion.40
  504.6 1.6 multiply_reduce_fusion
  506.3 4.3 broadcast_in_dim.14
  510.6 3.9 all-to-all-start.1
  514.5 11.4 %all-to-all-done.1 = f32[2,1,186368]{2,1,0:T(1,128)S(1)} async-done(((f32[2,1,186368]{2,1,0:T(1,128)}), f32[2,1,186368]{2,1,0:T(1,128)S(1)}, u32[]{:S(2)}, u32[]{:S(2)}) %all-to-all-start.1) | async-done | bytes 1490976 | tf_op jit(solution)/shard_map/all_to_all | solution.py:62
  526.0 7.0 %reduce_sum.53 = f32[186368]{0:T(1024)S(1)} reduce(f32[2,1,186368]{2,1,0:T(1,128)S(1)} %all-to-all-done.1, f32[]{:T(128)} %constant.43.clone.1), dimensions={0,1}, to_apply=%region_4.5 | reduce | flops 186368 | bytes 2236420 | tf_op jit(solution)/shard_map/reduce_sum | solution.py:66
  533.9 2.0 reshape.101
  (199 shorter events, 54.5 us)
Async XLA Ops:
  7.2 491.3 %copy-start = (bf16[1024,362]{0,1:T(8,128)(2,1)S(1)}, bf16[1024,362]{0,1:T(8,128)(2,1)}, u32[]{:S(2)}) copy-start(bf16[1024,362]{0,1:T(8,128)(2,1)} %param.22) | copy-start | bytes 2224132
  7.2 43.4 %all-gather.8.cloned.1.call-start = ((), (), s32[]{:S(2)}) async-start(), calls=%async_computation.3 | async-start | bytes 3145728 | tf_op jit(solution)/shard_map/all_gather | solution.py:101
  7.9 192.8 %all-gather.6.cloned.1.call-start = ((), (), s32[]{:S(2)}) async-start(), calls=%async_computation.2 | async-start | bytes 16908288 | tf_op jit(solution)/shard_map/all_gather | solution.py:105
  8.7 431.5 %all-gather.10.cloned.1.call-start = ((), (), s32[]{:S(2)}) async-start(), calls=%async_computation.4 | async-start | bytes 4227072 | tf_op jit(solution)/shard_map/all_gather | solution.py:130
  213.2 7.8 %copy-start.30 = (f32[1024]{0:T(1024)S(1)}, f32[1024]{0:T(1024)}, u32[]{:S(2)}) copy-start(f32[1024]{0:T(1024)} %param.20) | copy-start | bytes 12292
  216.1 1.3 copy-start.3
  217.5 9.5 %collective-permute-start = (f32[2,3,1024]{2,1,0:T(4,128)S(1)}, f32[2,3,1024]{2,1,0:T(4,128)S(1)}, u32[]{:S(2)}, u32[]{:S(2)}) collective-permute-start(f32[2,3,1024]{2,1,0:T(4,128)S(1)} %slice.415), channel_id=1, source_target_pairs={{0,16},{16,32},{32,48},{48,64},{64,80},{80,96},{96,112},{112,128},... | collective-permute-start | bytes 73736 | tf_op jit(solution)/shard_map/ppermute | solution.py:13
  335.2 10.0 %copy-start.17 = (f32[2,2,1024]{2,1,0:T(2,128)S(1)}, f32[2,2,1024]{2,1,0:T(2,128)}, u32[]{:S(2)}) copy-start(f32[2,2,1024]{2,1,0:T(2,128)} %get-tuple-element.178) | copy-start | bytes 49156
  335.2 10.1 %copy-start.16 = (f32[2,2,1024]{2,1,0:T(2,128)S(1)}, f32[2,2,1024]{2,1,0:T(2,128)}, u32[]{:S(2)}) copy-start(f32[2,2,1024]{2,1,0:T(2,128)} %get-tuple-element.177) | copy-start | bytes 49156
  335.2 10.1 %copy-start.25 = (f32[2,1,1024]{2,1,0:T(1,128)S(1)}, f32[2,1,1024]{2,1,0:T(1,128)}, u32[]{:S(2)}) copy-start(f32[2,1,1024]{2,1,0:T(1,128)} %get-tuple-element.159) | copy-start | bytes 24580
  335.2 10.1 %copy-start.26 = (f32[2,1,1024]{2,1,0:T(1,128)S(1)}, f32[2,1,1024]{2,1,0:T(1,128)}, u32[]{:S(2)}) copy-start(f32[2,1,1024]{2,1,0:T(1,128)} %get-tuple-element.160) | copy-start | bytes 24580
  335.2 10.2 %copy-start.27 = (f32[2,1,1024]{2,1,0:T(1,128)S(1)}, f32[2,1,1024]{2,1,0:T(1,128)}, u32[]{:S(2)}) copy-start(f32[2,1,1024]{2,1,0:T(1,128)} %get-tuple-element.161) | copy-start | bytes 24580
  335.2 10.2 %copy-start.28 = (f32[2,1,1024]{2,1,0:T(1,128)S(1)}, f32[2,1,1024]{2,1,0:T(1,128)}, u32[]{:S(2)}) copy-start(f32[2,1,1024]{2,1,0:T(1,128)} %get-tuple-element.162) | copy-start | bytes 24580
  335.2 10.3 %copy-start.15 = (f32[2,3,1024]{2,1,0:T(4,128)S(1)}, f32[2,3,1024]{2,1,0:T(4,128)}, u32[]{:S(2)}) copy-start(f32[2,3,1024]{2,1,0:T(4,128)} %slice.378) | copy-start | bytes 73732
  340.8 6.4 %copy-start.13 = (f32[2,7,1024]{2,1,0:T(8,128)S(1)}, f32[2,7,1024]{2,1,0:T(8,128)}, u32[]{:S(2)}) copy-start(f32[2,7,1024]{2,1,0:T(8,128)} %slice.355) | copy-start | bytes 172036
  340.8 6.4 %copy-start.14 = (f32[2,7,1024]{2,1,0:T(8,128)S(1)}, f32[2,7,1024]{2,1,0:T(8,128)}, u32[]{:S(2)}) copy-start(f32[2,7,1024]{2,1,0:T(8,128)} %slice.380) | copy-start | bytes 172036
  343.8 5.2 copy-start.12
  346.4 2.7 copy-start.24
  347.3 2.0 copy-start.23
  349.0 1.0 copy-start.10
  349.1 1.0 copy-start.11
  349.4 0.8 copy-start.22
  350.1 0.7 copy-start.21
  350.9 1.2 copy-start.8
  350.9 1.4 copy-start.9
  352.3 1.2 copy-start.20
  356.1 5.4 copy-start.19
  368.4 2.9 copy-start.1
  368.4 2.9 copy-start.2
  368.4 2.9 copy-start.6
  371.3 2.9 copy-start.18
  375.3 5.4 copy-start.4
  447.0 5.8 %copy-start.31 = (bf16[1024]{0:T(1024)(128)(2,1)S(1)}, bf16[1024]{0:T(1024)(128)(2,1)}, u32[]{:S(2)}) copy-start(bf16[1024]{0:T(1024)(128)(2,1)} %param.23) | copy-start | bytes 6148
  447.0 46.1 %all-to-all-start = ((f32[2,512,1024]{2,1,0:T(8,128)}), f32[2,512,1024]{2,1,0:T(8,128)}, u32[]{:S(2)}, u32[]{:S(2)}) async-start(f32[2,512,1024]{2,1,0:T(8,128)} %convolution_bitcast_fusion.1), calls=%async_computation | async-start | bytes 8388608 | tf_op jit(solution)/shard_map/all_to_all | solution.py:56
  497.5 1.0 copy-start.5
  502.9 3.3 copy-start.7
  506.2 8.2 %copy-start.32 = (s32[2,256]{1,0:T(2,128)S(1)}, s32[2,256]{1,0:T(2,128)}, u32[]{:S(2)}) copy-start(s32[2,256]{1,0:T(2,128)} %param.13) | copy-start | bytes 6148
  506.3 8.3 %copy-start.34 = (s32[2]{0:T(128)S(1)}, s32[2]{0:T(128)}, u32[]{:S(2)}) copy-start(s32[2]{0:T(128)} %param.15) | copy-start | bytes 28
  510.6 15.4 %all-to-all-start.1 = ((f32[2,1,186368]{2,1,0:T(1,128)}), f32[2,1,186368]{2,1,0:T(1,128)S(1)}, u32[]{:S(2)}, u32[]{:S(2)}) async-start(f32[2,1,186368]{2,1,0:T(1,128)} %broadcast_in_dim.14), calls=%async_computation.1 | async-start | bytes 2981888 | tf_op jit(solution)/shard_map/all_to_all | solution.py:62
  532.9 3.7 copy-start.33
  536.6 0.7 copy-start.29
Sparse Core Ops, SparseCore 0:
  9.8 40.6 all-gather.7
  54.2 146.4 all-gather.5
  204.4 115.7 all-gather.9
where the time goes:
time: 547 us; the launch traced here: 544 us
  waiting for transfers between devices  249 us (46%)
  local copies, waits for them, and re-layouts  142 us (26%)
  other arithmetic  64 us (12%)
  blocking collectives  37.9 us (7%)
  matrix products  22.7 us (4%)
  between operations  14.6 us (3%)
  starting transfers between devices  13.3 us (2%)
    all_gather x1, waiting for transfers between devices, shards(): lax.all_gather(w_branches, ('tm', 'batch'), axis=1, tiled=True)  150 us
    slice x52, local copies, waits for them, and re-layouts, shards(): summed, local = lax.associative_scan(link, (log_a, drive), axis=1)  94.2 us
    all_to_all x1, waiting for transfers between devices, sum_at_owner(): pieces = lax.all_to_all(in_blocks(x, dim, length), axis, 0, 0, tiled=True)  40.3 us
    all_gather x1, waiting for transfers between devices, shards(): lax.all_gather(embedded, 'width', axis=2, tiled=True).reshape(count, -1)  39.5 us
    all_gather x1, blocking collectives, collected_together(): both, at, found = (lax.all_gather(jnp.concatenate(lines), axis), 0, {})  37.9 us
    pad x28, local copies, waits for them, and re-layouts, shards(): summed, local = lax.associative_scan(link, (log_a, drive), axis=1)  29.1 us
    add x13, other arithmetic, link(): return (early[0] + late[0], jnp.exp(late[0]) * early[1] + late[1])  18.5 us
    dot_general x1, matrix products, shards(): jnp.einsum('td,kdn->ktn', features, lax.all_gather(w_branches, ('tm', 'ba...  12.5 us
  transfers between devices with their start and end apart: 6, of which 5 were waited for; matrix products, arithmetic and copies ran while one was open for 35% of the time, Pallas kernels for 0%

commit v1 on v0

--- a/solution.py
+++ b/solution.py
@@ -98,7 +98,9 @@
     games, block_len, half = embedded.shape
     count = games * block_len
     chans = w_branches.shape[2]
-    features = lax.all_gather(embedded, "width", axis=2, tiled=True).reshape(count, -1)
+    features = jnp.concatenate(
+        lax.all_to_all(jnp.stack([embedded] * lax.axis_size("width")), "width", 0, 0), axis=2
+    ).reshape(count, -1)
     proj = jnp.einsum(
         "td,kdn->ktn",
         features,

time: 547 us -> 506 us (0.925)
  waiting for transfers between devices: 249 us -> 196 us
    all_gather x1 -> x0, waiting for transfers between devices: 39.5 us -> none  [shards(): lax.all_gather(embedded, 'width', axis=2, tiled=True).reshape(count, -1)]
    all_gather x1, waiting for transfers between devices: 150 us -> 112 us  [shards(): lax.all_gather(w_branches, ('tm', 'batch'), axis=1, tiled=True)]
    all_to_all x0 -> x1, waiting for transfers between devices: none -> 25.2 us  [shards(): lax.all_to_all(jnp.stack([embedded] * lax.axis_size('width')), 'width', 0...]
  transfers between devices with their start and end apart: 6 -> 6, of which waited for: 5 -> 5; matrix products, arithmetic and copies ran while one was open for 35% -> 39% of each run, Pallas kernels for 0% -> 0%
where the time goes in v1:
time: 506 us; the launch traced here: 502 us
  waiting for transfers between devices  196 us (39%)
  local copies, waits for them, and re-layouts  147 us (29%)
  other arithmetic  67.2 us (13%)
  blocking collectives  37.8 us (7%)
  matrix products  22 us (4%)
  starting transfers between devices  17.2 us (3%)
  between operations  14.9 us (3%)
    all_gather x1, waiting for transfers between devices, shards(): lax.all_gather(w_branches, ('tm', 'batch'), axis=1, tiled=True)  112 us
    slice x52, local copies, waits for them, and re-layouts, shards(): summed, local = lax.associative_scan(link, (log_a, drive), axis=1)  93.9 us
    all_to_all x1, waiting for transfers between devices, sum_at_owner(): pieces = lax.all_to_all(in_blocks(x, dim, length), axis, 0, 0, tiled=True)  39.8 us
    all_gather x1, blocking collectives, collected_together(): both, at, found = (lax.all_gather(jnp.concatenate(lines), axis), 0, {})  37.8 us
    pad x28, local copies, waits for them, and re-layouts, shards(): summed, local = lax.associative_scan(link, (log_a, drive), axis=1)  29.2 us
    all_to_all x1, waiting for transfers between devices, shards(): lax.all_to_all(jnp.stack([embedded] * lax.axis_size('width')), 'width', 0...  25.2 us
    add x13, other arithmetic, link(): return (early[0] + late[0], jnp.exp(late[0]) * early[1] + late[1])  18.5 us
    dot_general x1, matrix products, shards(): jnp.einsum('td,kdn->ktn', features, lax.all_gather(w_branches, ('tm', 'ba...  11.8 us
  transfers between devices with their start and end apart: 6, of which 5 were waited for; matrix products, arithmetic and copies ran while one was open for 39% of the time, Pallas kernels for 0%

profile of v1, /device:TPU:16, one launch (start us, length us, event | category | flops | bytes accessed | tf_op | source)
XLA Modules:
  0.0 501.7 jit_solution(8444963284167334614)
XLA Ops:
  7.9 3.2 pad_maximum_fusion.1
  11.1 3.9 all-to-all-start
  15.8 25.2 %all-to-all-done = bf16[2,2,256,1024]{3,2,1,0:T(8,128)(2,1)S(1)} async-done(((bf16[2,2,256,1024]{3,2,1,0:T(8,128)(2,1)}), bf16[2,2,256,1024]{3,2,1,0:T(8,128)(2,1)S(1)}, u32[]{:S(2)}, u32[]{:S(2)}) %all-to-all-start) | async-done | bytes 2097184 | tf_op jit(solution)/shard_map/all_to_all | solution.py:102
  41.0 3.5 copy.33
  44.6 3.3 reshape.108
  47.8 112.0 %all-gather.5.cloned.1.call-done = bf16[4,2048,1024]{2,1,0:T(8,128)(2,1)} async-done(((bf16[4,16,1024]{2,1,0:T(8,128)(2,1)}), bf16[4,2048,1024]{2,1,0:T(8,128)(2,1)}) %all-gather.5.cloned.1.call-update) | async-done | bytes 16777232 | tf_op jit(solution)/shard_map/all_gather | solution.py:107
  159.8 11.8 %convolution_bitcast_fusion = f32[4,512,1024]{2,1,0:T(8,128)S(1)} fusion(bf16[512,2048,1]{1,0,2:T(8,128)(2,1)S(1)} %reshape.108, bf16[4,2048,1024]{2,1,0:T(8,128)(2,1)} %all-gather.5.cloned.1.call-done), kind=kOutput, calls=%fused_computation.3 | convolution fusion | flops 8589934592 | bytes 27262976 | tf_op jit(solution)/shard_map/td,kdn->ktn/dot_general | solution.py:104
  171.6 2.9 fusion.33
  175.9 3.5 collective-permute-start
  179.4 5.9 %collective-permute-done = f32[2,3,1024]{2,1,0:T(4,128)S(1)} collective-permute-done((f32[2,3,1024]{2,1,0:T(4,128)S(1)}, f32[2,3,1024]{2,1,0:T(4,128)S(1)}, u32[]{:S(2)}, u32[]{:S(2)}) %collective-permute-start) | collective-permute-done | bytes 24608 | tf_op jit(solution)/shard_map/ppermute | solution.py:13
  185.3 7.6 %fusion.5 = (f32[2,256,1024]{2,1,0:T(8,128)S(1)}, f32[2,256,1024]{2,1,0:T(8,128)}) fusion(f32[2,3,1024]{2,1,0:T(4,128)S(1)} %collective-permute-done, f32[2,256,1024]{2,1,0:T(8,128)} %bitcast.67, f32[2,256,1024]{2,1,0:T(8,128)} %bitcast.71, f32[1024]{0:T(1024)S(1)} %bitcast.89, f32[1024]{0:T(1024)S(1)} %bitcast.90, f32[1024]{0:T(1024)S(1)} %bitcast.88, ...), kind=kLoop, calls=%fused_computation.12 | loop fusion | flops 12058624 | bytes 10539008 | tf_op jit(solution)/shard_map/mul | solution.py:122
  192.9 2.8 slice.333
  195.7 2.9 slice.334
  198.6 5.4 %slice.332 = f32[2,128,1024]{2,1,0:T(8,128)} slice(f32[2,256,1024]{2,1,0:T(8,128)} %get-tuple-element.128), slice={[0:2:1], [1:256:2], [0:1024:1]} | slice | bytes 2097152 | tf_op jit(solution)/shard_map/slice | solution.py:123
  204.0 5.4 %slice.336 = f32[2,128,1024]{2,1,0:T(8,128)} slice(f32[2,256,1024]{2,1,0:T(8,128)} %get-tuple-element.128), slice={[0:2:1], [0:255:2], [0:1024:1]} | slice | bytes 2097152 | tf_op jit(solution)/shard_map/slice | solution.py:123
  209.4 4.1 multiply_add_fusion
  213.5 3.2 slice.339
  216.7 3.2 slice.340
  220.0 3.3 slice.338
  223.2 3.3 slice.342
  226.5 2.5 multiply_add_fusion.1
  230.5 1.7 slice.344
  232.2 1.7 slice.348
  233.9 2.0 multiply_add_fusion.2
  235.9 1.6 slice.351
  237.6 1.6 slice.352
  239.2 1.6 slice.350
  240.8 1.6 slice.354
  242.4 1.8 multiply_add_fusion.3
  247.0 1.5 slice.360
  248.5 1.7 multiply_add_fusion.4
  269.6 1.5 slice.355
  274.8 1.6 slice.382
  279.3 1.7 slice.343
  283.9 3.3 slice.337
  287.2 3.3 slice.386
  293.4 5.6 %slice.331 = f32[2,127,1024]{2,1,0:T(8,128)} slice(f32[2,256,1024]{2,1,0:T(8,128)} %get-tuple-element.128), slice={[0:2:1], [2:256:2], [0:1024:1]} | slice | bytes 2080768 | tf_op jit(solution)/shard_map/slice | solution.py:123
  298.9 2.9 slice.388
  314.2 5.4 %pad.129 = f32[2,256,1024]{2,1,0:T(8,128)} pad(f32[2,128,1024]{2,1,0:T(8,128)} %add.362, f32[]{:T(128)} %constant.43.clone.1), padding=0_0_0x1_0_1x0_0_0 | pad | bytes 3145732 | tf_op jit(solution)/shard_map/pad | solution.py:123
  319.5 2.0 pad_maximum_fusion.5
  321.5 3.0 pad.110
  324.5 2.0 pad.111
  326.5 2.9 add.346
  329.4 2.9 fusion.20
  333.4 5.4 %pad.128 = f32[2,256,1024]{2,1,0:T(8,128)} pad(f32[2,128,1024]{2,1,0:T(8,128)} %pad_maximum_fusion.3, f32[]{:T(128)} %constant.43.clone.1), padding=0_0_0x0_1_1x0_0_0 | pad | bytes 3145732 | tf_op jit(solution)/shard_map/pad | solution.py:123
  339.7 5.4 %pad.113 = f32[2,256,1024]{2,1,0:T(8,128)} pad(f32[2,128,1024]{2,1,0:T(8,128)} %add.346, f32[]{:T(128)} %constant.43.clone.1), padding=0_0_0x1_0_1x0_0_0 | pad | bytes 3145732 | tf_op jit(solution)/shard_map/pad | solution.py:123
  345.1 2.3 pad_maximum_fusion.2
  347.4 5.5 %pad.112 = f32[2,256,1024]{2,1,0:T(8,128)} pad(f32[2,128,1024]{2,1,0:T(8,128)} %pad_maximum_fusion.2, f32[]{:T(128)} %constant.43.clone.1), padding=0_0_0x0_1_1x0_0_0 | pad | bytes 3145732 | tf_op jit(solution)/shard_map/pad | solution.py:123
  353.8 37.8 %all-gather.1 = f32[16,4,1024]{2,1,0:T(4,128)S(1)} all-gather(f32[1,4,1024]{2,1,0:T(4,128)S(1)} %maximum_bitcast_fusion), channel_id=2, replica_groups=mesh['tm'=16,'batch'=8,'width'=2] {'tm'}, dimensions={0}, use_global_device_ids=true | all-gather | bytes 278528 | tf_op jit(solution)/shard_map/all_gather | solution.py:24
  392.4 5.8 %fusion.17 = bf16[2,256,1024]{2,1,0:T(8,128)(2,1)} fusion(f32[2,256,1024]{2,1,0:T(8,128)} %bitcast.69, f32[2,256,1024]{2,1,0:T(8,128)} %pad.128, f32[2,256,1024]{2,1,0:T(8,128)S(1)} %copy-done.4, f32[2,256,1024]{2,1,0:T(8,128)} %pad.112, f32[2,256,1024]{2,1,0:T(8,128)} %pad.113, f32[2,1024]{1,0:T(2,128)S(1)} %get-tuple-element.96), kind=kLoop, calls=%fused_computation.24 | loop fusion | flops 7340032 | bytes 11542528 | tf_op jit(solution)/shard_map/convert_element_type | solution.py:129
  398.2 6.9 %convolution_bitcast_fusion.1 = f32[2,512,1024]{2,1,0:T(8,128)} fusion(bf16[512,1024,1]{1,0,2:T(8,128)(2,1)} %bitcast.72, bf16[2,1024,1024]{2,1,0:T(8,128)(2,1)} %bitcast.96), kind=kOutput, calls=%fused_computation.7 | convolution fusion | flops 2147483648 | bytes 9437184 | tf_op jit(solution)/shard_map/dot_general | solution.py:130
  405.1 5.8 %all-to-all-start.1 = ((f32[2,512,1024]{2,1,0:T(8,128)}), f32[2,512,1024]{2,1,0:T(8,128)}, u32[]{:S(2)}, u32[]{:S(2)}) async-start(f32[2,512,1024]{2,1,0:T(8,128)} %convolution_bitcast_fusion.1), calls=%async_computation.1 | async-start | bytes 8388608 | tf_op jit(solution)/shard_map/all_to_all | solution.py:56
  410.9 39.8 %all-to-all-done.1 = f32[2,512,1024]{2,1,0:T(8,128)} async-done(((f32[2,512,1024]{2,1,0:T(8,128)}), f32[2,512,1024]{2,1,0:T(8,128)}, u32[]{:S(2)}, u32[]{:S(2)}) %all-to-all-start.1) | async-done | bytes 4194336 | tf_op jit(solution)/shard_map/all_to_all | solution.py:56
  450.6 2.8 reduce_sum.49
  453.4 1.6 fusion.19
  456.0 1.6 fusion.39
  457.6 2.8 reshape.100
  460.5 1.7 fusion.40
  462.1 1.6 multiply_reduce_fusion
  463.8 4.3 broadcast_in_dim.14
  468.1 3.9 all-to-all-start.2
  472.1 11.4 %all-to-all-done.2 = f32[2,1,186368]{2,1,0:T(1,128)S(1)} async-done(((f32[2,1,186368]{2,1,0:T(1,128)}), f32[2,1,186368]{2,1,0:T(1,128)S(1)}, u32[]{:S(2)}, u32[]{:S(2)}) %all-to-all-start.2) | async-done | bytes 1490976 | tf_op jit(solution)/shard_map/all_to_all | solution.py:62
  483.5 7.0 %reduce_sum.53 = f32[186368]{0:T(1024)S(1)} reduce(f32[2,1,186368]{2,1,0:T(1,128)S(1)} %all-to-all-done.2, f32[]{:T(128)} %constant.43.clone.1), dimensions={0,1}, to_apply=%region_4.5 | reduce | flops 186368 | bytes 2236420 | tf_op jit(solution)/shard_map/reduce_sum | solution.py:66
  491.4 2.0 reshape.101
  (205 shorter events, 58.1 us)
Async XLA Ops:
  7.2 448.9 %copy-start = (bf16[1024,362]{0,1:T(8,128)(2,1)S(1)}, bf16[1024,362]{0,1:T(8,128)(2,1)}, u32[]{:S(2)}) copy-start(bf16[1024,362]{0,1:T(8,128)(2,1)} %param.22) | copy-start | bytes 2224132
  7.2 152.6 %all-gather.5.cloned.1.call-start = ((), (), s32[]{:S(2)}) async-start(), calls=%async_computation.3 | async-start | bytes 16908288 | tf_op jit(solution)/shard_map/all_gather | solution.py:107
  11.1 4.7 copy-start.30
  11.1 4.7 copy-start.29
  11.1 30.0 %all-to-all-start = ((bf16[2,2,256,1024]{3,2,1,0:T(8,128)(2,1)}), bf16[2,2,256,1024]{3,2,1,0:T(8,128)(2,1)S(1)}, u32[]{:S(2)}, u32[]{:S(2)}) async-start(bf16[2,2,256,1024]{3,2,1,0:T(8,128)(2,1)} %pad_maximum_fusion.1), calls=%async_computation | async-start | bytes 4194304 | tf_op jit(solution)/shard_map/all_to_all | solution.py:102
  15.0 383.2 %all-gather.7.cloned.1.call-start = ((), (), s32[]{:S(2)}) async-start(), calls=%async_computation.4 | async-start | bytes 4227072 | tf_op jit(solution)/shard_map/all_gather | solution.py:132
  171.6 7.8 %copy-start.32 = (f32[1024]{0:T(1024)S(1)}, f32[1024]{0:T(1024)}, u32[]{:S(2)}) copy-start(f32[1024]{0:T(1024)} %param.20) | copy-start | bytes 12292
  174.5 1.3 copy-start.3
  175.9 9.4 %collective-permute-start = (f32[2,3,1024]{2,1,0:T(4,128)S(1)}, f32[2,3,1024]{2,1,0:T(4,128)S(1)}, u32[]{:S(2)}, u32[]{:S(2)}) collective-permute-start(f32[2,3,1024]{2,1,0:T(4,128)S(1)} %slice.415), channel_id=1, source_target_pairs={{0,16},{16,32},{32,48},{48,64},{64,80},{80,96},{96,112},{112,128},... | collective-permute-start | bytes 73736 | tf_op jit(solution)/shard_map/ppermute | solution.py:13
  293.3 10.0 %copy-start.17 = (f32[2,2,1024]{2,1,0:T(2,128)S(1)}, f32[2,2,1024]{2,1,0:T(2,128)}, u32[]{:S(2)}) copy-start(f32[2,2,1024]{2,1,0:T(2,128)} %get-tuple-element.178) | copy-start | bytes 49156
  293.3 10.1 %copy-start.16 = (f32[2,2,1024]{2,1,0:T(2,128)S(1)}, f32[2,2,1024]{2,1,0:T(2,128)}, u32[]{:S(2)}) copy-start(f32[2,2,1024]{2,1,0:T(2,128)} %get-tuple-element.177) | copy-start | bytes 49156
  293.3 10.1 %copy-start.25 = (f32[2,1,1024]{2,1,0:T(1,128)S(1)}, f32[2,1,1024]{2,1,0:T(1,128)}, u32[]{:S(2)}) copy-start(f32[2,1,1024]{2,1,0:T(1,128)} %get-tuple-element.159) | copy-start | bytes 24580
  293.3 10.1 %copy-start.26 = (f32[2,1,1024]{2,1,0:T(1,128)S(1)}, f32[2,1,1024]{2,1,0:T(1,128)}, u32[]{:S(2)}) copy-start(f32[2,1,1024]{2,1,0:T(1,128)} %get-tuple-element.160) | copy-start | bytes 24580
  293.3 10.1 %copy-start.27 = (f32[2,1,1024]{2,1,0:T(1,128)S(1)}, f32[2,1,1024]{2,1,0:T(1,128)}, u32[]{:S(2)}) copy-start(f32[2,1,1024]{2,1,0:T(1,128)} %get-tuple-element.161) | copy-start | bytes 24580
  293.3 10.1 %copy-start.28 = (f32[2,1,1024]{2,1,0:T(1,128)S(1)}, f32[2,1,1024]{2,1,0:T(1,128)}, u32[]{:S(2)}) copy-start(f32[2,1,1024]{2,1,0:T(1,128)} %get-tuple-element.162) | copy-start | bytes 24580
  293.3 10.3 %copy-start.15 = (f32[2,3,1024]{2,1,0:T(4,128)S(1)}, f32[2,3,1024]{2,1,0:T(4,128)}, u32[]{:S(2)}) copy-start(f32[2,3,1024]{2,1,0:T(4,128)} %slice.378) | copy-start | bytes 73732
  298.9 6.4 %copy-start.13 = (f32[2,7,1024]{2,1,0:T(8,128)S(1)}, f32[2,7,1024]{2,1,0:T(8,128)}, u32[]{:S(2)}) copy-start(f32[2,7,1024]{2,1,0:T(8,128)} %slice.355) | copy-start | bytes 172036
  298.9 6.4 %copy-start.14 = (f32[2,7,1024]{2,1,0:T(8,128)S(1)}, f32[2,7,1024]{2,1,0:T(8,128)}, u32[]{:S(2)}) copy-start(f32[2,7,1024]{2,1,0:T(8,128)} %slice.380) | copy-start | bytes 172036
  301.8 5.2 %copy-start.12 = (f32[2,15,1024]{2,1,0:T(8,128)S(1)}, f32[2,15,1024]{2,1,0:T(8,128)}, u32[]{:S(2)}) copy-start(f32[2,15,1024]{2,1,0:T(8,128)} %slice.382) | copy-start | bytes 368644
  304.4 2.7 copy-start.24
  305.4 2.0 copy-start.23
  307.1 1.0 copy-start.10
  307.1 1.0 copy-start.11
  307.4 0.8 copy-start.22
  308.2 0.7 copy-start.21
  309.0 1.2 copy-start.8
  309.0 1.4 copy-start.9
  310.4 1.2 copy-start.20
  314.2 5.4 %copy-start.19 = (f32[2,1,1024]{2,1,0:T(1,128)S(1)}, f32[2,1,1024]{2,1,0:T(1,128)}, u32[]{:S(2)}) copy-start(f32[2,1,1024]{2,1,0:T(1,128)} %slice.421) | copy-start | bytes 24580
  326.5 2.9 copy-start.1
  326.5 2.9 copy-start.2
  326.5 2.9 copy-start.6
  329.4 2.9 copy-start.18
  333.4 5.4 %copy-start.4 = (f32[2,256,1024]{2,1,0:T(8,128)S(1)}, f32[2,256,1024]{2,1,0:T(8,128)}, u32[]{:S(2)}) copy-start(f32[2,256,1024]{2,1,0:T(8,128)} %pad.129) | copy-start | bytes 6291460
  405.1 5.8 %copy-start.33 = (bf16[1024]{0:T(1024)(128)(2,1)S(1)}, bf16[1024]{0:T(1024)(128)(2,1)}, u32[]{:S(2)}) copy-start(bf16[1024]{0:T(1024)(128)(2,1)} %param.23) | copy-start | bytes 6148
  405.1 45.6 %all-to-all-start.1 = ((f32[2,512,1024]{2,1,0:T(8,128)}), f32[2,512,1024]{2,1,0:T(8,128)}, u32[]{:S(2)}, u32[]{:S(2)}) async-start(f32[2,512,1024]{2,1,0:T(8,128)} %convolution_bitcast_fusion.1), calls=%async_computation.1 | async-start | bytes 8388608 | tf_op jit(solution)/shard_map/all_to_all | solution.py:56
  455.0 1.0 copy-start.5
  460.5 3.3 copy-start.7
  463.8 8.2 %copy-start.34 = (s32[2,256]{1,0:T(2,128)S(1)}, s32[2,256]{1,0:T(2,128)}, u32[]{:S(2)}) copy-start(s32[2,256]{1,0:T(2,128)} %param.13) | copy-start | bytes 6148
  463.8 8.3 %copy-start.36 = (s32[2]{0:T(128)S(1)}, s32[2]{0:T(128)}, u32[]{:S(2)}) copy-start(s32[2]{0:T(128)} %param.15) | copy-start | bytes 28
  468.1 15.4 %all-to-all-start.2 = ((f32[2,1,186368]{2,1,0:T(1,128)}), f32[2,1,186368]{2,1,0:T(1,128)S(1)}, u32[]{:S(2)}, u32[]{:S(2)}) async-start(f32[2,1,186368]{2,1,0:T(1,128)} %broadcast_in_dim.14), calls=%async_computation.2 | async-start | bytes 2981888 | tf_op jit(solution)/shard_map/all_to_all | solution.py:62
  490.5 3.7 copy-start.35
  494.2 0.7 copy-start.31
Sparse Core Ops, SparseCore 0:
  11.7 148.1 all-gather.4
  163.5 115.7 all-gather.6
